TPU v7x, 512 devices: a whole 4x4x16 slice. The times are simulated.
512 devices in a mesh: dp: 32 (over y, z_lo), tensor: 16 (over x, z_hi, core).
Axes of the slice: x: 4, y: 4, z: 16 (z_hi: 2, z_lo: 8; z = z_hi * 8 + z_lo), core: 2. Of those that a mesh axis runs over, the one named last changes fastest.
Arguments:
- tokens: bfloat16 [16384, 4096], P(('dp', 'tensor')), may hold values from -6 to 6
- weight: bfloat16 [4096, 4096], P('tensor', 'dp'), may hold values from -0.09375 to 0.09375
Outputs:
- projected: bfloat16 [16384, 4096], P('dp', 'tensor')
All inputs are finite; a program needn't handle non-finite values.
Results may differ from a plain program's by a relative error of at most 0.0057.
Values may be sent and summed in bfloat16 or wider, within the bound.
A program may use at most 64 MiB of HBM per device.

v0:
```python
import jax
import jax.numpy as jnp
from jax import lax
from jax.sharding import PartitionSpec as P


def contract_last(left, right):
    return lax.dot_general(
        left, right, (((1,), (1,)), ((), ())), preferred_element_type=jnp.float32
    )


def contract_first(left, right):
    return lax.dot_general(
        left, right, (((0,), (0,)), ((), ())), preferred_element_type=jnp.float32
    )


def on_device(tokens, weight):
    col_slab = lax.all_gather(weight, "tensor", axis=0, tiled=True)
    term = contract_last(col_slab, weight)
    gram_cols = lax.psum(term, "dp").astype(jnp.bfloat16)
    update = 1.5 * weight.astype(jnp.float32) - 0.5 * contract_first(gram_cols, col_slab)
    ortho = update.astype(jnp.bfloat16)
    full_rows = lax.all_gather(ortho, "dp", axis=1, tiled=True)
    result = contract_last(lax.all_gather(tokens, "tensor", axis=0, tiled=True), full_rows)
    return result.astype(jnp.bfloat16)


def solution(mesh):
    placed = (P(("dp", "tensor"), None), P("tensor", "dp"))
    return jax.shard_map(
        on_device, mesh=mesh, in_specs=placed, out_specs=P("dp", "tensor"), check_vma=False
    )
```

profile of v0, /device:TPU:1, one launch (start us, length us, event | category | flops | bytes accessed | tf_op | source)
XLA Modules:
  0.0 695.2 jit_solution(15658774399451351064)
XLA Ops:
  6.5 0.0 all-gather.4.cloned.1.call-start
  6.5 0.7 all-gather.4.cloned.1.call-update
  7.3 0.0 all-gather.6.cloned.1.call-start
  7.3 86.7 %all-gather.4.cloned.1.call-done = bf16[4096,128]{1,0:T(8,128)(2,1)} async-done(((bf16[256,128]{1,0:T(8,128)(2,1)}), bf16[4096,128]{1,0:T(8,128)(2,1)}) %all-gather.4.cloned.1.call-update) | async-done | bytes 1048592 | tf_op jit(solution)/shard_map/all_gather | solution.py:20
  94.0 3.9 fusion.12
  97.9 0.0 copy-start
  97.9 0.0 copy-start.1
  97.9 255.6 %all-reduce.1 = bf16[4096,256]{1,0:T(8,128)(2,1)S(1)} all-reduce(f32[4096,256]{1,0:T(8,128)} %fusion.12), channel_id=1, replica_groups=mesh['dp'=32,'tensor'=16] {'dp'}, use_global_device_ids=true, to_apply=%region_0.0 | all-reduce | flops 1048576 | bytes 6291456 | tf_op jit(solution)/shard_map/psum | solution.py:22
  353.5 0.0 copy-done
  353.5 0.0 copy-done.1
  353.5 1.4 fusion.9
  354.9 0.0 all-gather.6.cloned.1.call-update
  354.9 0.0 all-gather.8.cloned.1.call-start
  354.9 0.7 all-gather.8.cloned.1.call-update
  355.6 193.9 %all-gather.6.cloned.1.call-done = bf16[256,4096]{1,0:T(8,128)(2,1)} async-done(((bf16[256,128]{1,0:T(8,128)(2,1)}), bf16[256,4096]{1,0:T(8,128)(2,1)}) %all-gather.6.cloned.1.call-update) | async-done | bytes 2097168 | tf_op jit(solution)/shard_map/all_gather | solution.py:25
  549.5 134.2 %all-gather.8.cloned.1.call-done = bf16[512,4096]{1,0:T(8,128)(2,1)} async-done(((bf16[32,4096]{1,0:T(8,128)(2,1)}), bf16[512,4096]{1,0:T(8,128)(2,1)}) %all-gather.8.cloned.1.call-update) | async-done | bytes 4194320 | tf_op jit(solution)/shard_map/all_gather | solution.py:26
  683.7 4.1 fusion.2
  687.9 0.8 copy.3
Async XLA Ops:
  6.5 87.5 %all-gather.4.cloned.1.call-start = ((), (), s32[]{:S(2)}) async-start(), calls=%async_computation | async-start | bytes 1114112 | tf_op jit(solution)/shard_map/all_gather | solution.py:20
  7.3 542.3 %all-gather.6.cloned.1.call-start = ((), (), s32[]{:S(2)}) async-start(), calls=%async_computation.1 | async-start | bytes 2162688 | tf_op jit(solution)/shard_map/all_gather | solution.py:25
  97.9 255.6 %copy-start = (bf16[4096,128]{1,0:T(8,128)(2,1)S(1)}, bf16[4096,128]{1,0:T(8,128)(2,1)}, u32[]{:S(2)}) copy-start(bf16[4096,128]{1,0:T(8,128)(2,1)} %all-gather.4.cloned.1.call-done) | copy-start | bytes 3145732
  97.9 255.6 %copy-start.1 = (bf16[256,128]{1,0:T(8,128)(2,1)S(1)}, bf16[256,128]{1,0:T(8,128)(2,1)}, u32[]{:S(2)}) copy-start(bf16[256,128]{1,0:T(8,128)(2,1)} %param.3) | copy-start | bytes 196612
  354.9 328.9 %all-gather.8.cloned.1.call-start = ((), (), s32[]{:S(2)}) async-start(), calls=%async_computation.2 | async-start | bytes 4456448 | tf_op jit(solution)/shard_map/all_gather | solution.py:26
Sparse Core Ops, SparseCore 0:
  10.6 83.3 all-gather.3
  355.0 194.4 all-gather.5
  552.8 130.8 all-gather.7
where the time goes:
time: 695 us
  waiting for transfers between devices  416 us (60%)
  blocking collectives  256 us (37%)
  between operations  13.1 us (2%)
  matrix products  9.36 us (1%)
    psum x1, blocking collectives, on_device(): gram_cols = lax.psum(term, 'dp').astype(jnp.bfloat16)  256 us
    all_gather x1, waiting for transfers between devices, on_device(): full_rows = lax.all_gather(ortho, 'dp', axis=1, tiled=True)  194 us
    all_gather x1, waiting for transfers between devices, on_device(): lax.all_gather(tokens, 'tensor', axis=0, tiled=True)  134 us
    all_gather x1, waiting for transfers between devices, on_device(): col_slab = lax.all_gather(weight, 'tensor', axis=0, tiled=True)  86.7 us
  transfers between devices with their start and end apart: 3, of which 3 were waited for; matrix products, arithmetic and copies ran while one was open for 0% of the time, Pallas kernels for 0%

commit v1 on v0

--- a/solution.py
+++ b/solution.py
@@ -23,7 +23,13 @@
     update = 1.5 * weight.astype(jnp.float32) - 0.5 * contract_first(gram_cols, col_slab)
     ortho = update.astype(jnp.bfloat16)
     full_rows = lax.all_gather(ortho, "dp", axis=1, tiled=True)
-    result = contract_last(lax.all_gather(tokens, "tensor", axis=0, tiled=True), full_rows)
+
+    def do_the_streams(frame, dim_i):
+        e_next = jnp.stack([frame for _ in range(lax.axis_size("tensor"))])
+        e_now = lax.all_to_all(e_next, axis_name="tensor", split_axis=0, concat_axis=0)
+        return jnp.concatenate(e_now, dim_i)
+
+    result = contract_last(do_the_streams(tokens, 0), full_rows)
     return result.astype(jnp.bfloat16)
 
 

time: 695 us -> 735 us (1.058)
  the two profiles are of different devices: /device:TPU:1 before, /device:TPU:2 now
where the time goes in v1:
time: 735 us
  waiting for transfers between devices  380 us (52%)
  blocking collectives  310 us (42%)
  starting transfers between devices  18.3 us (2%)
  between operations  13.4 us (2%)
  matrix products  9.39 us (1%)
    psum x1, blocking collectives, on_device(): gram_cols = lax.psum(term, 'dp').astype(jnp.bfloat16)  310 us
    all_gather x1, waiting for transfers between devices, on_device(): full_rows = lax.all_gather(ortho, 'dp', axis=1, tiled=True)  191 us
    all_gather x1, waiting for transfers between devices, on_device(): col_slab = lax.all_gather(weight, 'tensor', axis=0, tiled=True)  188 us
    all_to_all x1, starting transfers between devices, do_the_streams(): lax.all_to_all(e_next, axis_name='tensor', split_axis=0, concat_axis=0)  18.2 us
  transfers between devices with their start and end apart: 3, of which 2 were waited for; matrix products, arithmetic and copies ran while one was open for 1% of the time, Pallas kernels for 0%

profile of v1, /device:TPU:2, one launch (start us, length us, event | category | flops | bytes accessed | tf_op | source)
XLA Modules:
  0.0 734.6 jit_solution(15140792650123389097)
XLA Ops:
  6.5 3.4 stack.2
  10.0 0.0 copy-start.1
  10.0 18.2 %all-to-all-start = ((bf16[16,32,4096]{2,1,0:T(8,128)(2,1)}), bf16[16,32,4096]{2,1,0:T(8,128)(2,1)}, u32[]{:S(2)}, u32[]{:S(2)}) async-start(bf16[16,32,4096]{2,1,0:T(8,128)(2,1)} %stack.2), calls=%async_computation | async-start | bytes 8388608 | tf_op jit(solution)/shard_map/all_to_all | solution.py:29
  28.2 0.0 all-gather.3.cloned.1.call-start
  28.3 0.7 all-gather.3.cloned.1.call-update
  28.9 0.0 all-gather.5.cloned.1.call-start
  29.0 188.3 %all-gather.3.cloned.1.call-done = bf16[4096,128]{1,0:T(8,128)(2,1)} async-done(((bf16[256,128]{1,0:T(8,128)(2,1)}), bf16[4096,128]{1,0:T(8,128)(2,1)}) %all-gather.3.cloned.1.call-update) | async-done | bytes 1048592 | tf_op jit(solution)/shard_map/all_gather | solution.py:20
  217.3 0.0 copy-done.1
  217.3 3.9 fusion.12
  221.2 0.0 copy-start
  221.2 309.7 %all-reduce.1 = bf16[4096,256]{1,0:T(8,128)(2,1)S(1)} all-reduce(f32[4096,256]{1,0:T(8,128)} %fusion.12), channel_id=1, replica_groups=mesh['dp'=32,'tensor'=16] {'dp'}, use_global_device_ids=true, to_apply=%region_0.0 | all-reduce | flops 1048576 | bytes 6291456 | tf_op jit(solution)/shard_map/psum | solution.py:22
  530.9 0.0 copy-done
  530.9 1.4 fusion.9
  532.3 0.0 all-gather.5.cloned.1.call-update
  532.3 190.5 %all-gather.5.cloned.1.call-done = bf16[256,4096]{1,0:T(8,128)(2,1)} async-done(((bf16[256,128]{1,0:T(8,128)(2,1)}), bf16[256,4096]{1,0:T(8,128)(2,1)}) %all-gather.5.cloned.1.call-update) | async-done | bytes 2097168 | tf_op jit(solution)/shard_map/all_gather | solution.py:25
  722.8 0.0 all-to-all-done
  722.8 4.1 fusion.2
  726.9 0.8 copy.3
Async XLA Ops:
  10.0 207.3 %copy-start.1 = (bf16[256,128]{1,0:T(8,128)(2,1)S(1)}, bf16[256,128]{1,0:T(8,128)(2,1)}, u32[]{:S(2)}) copy-start(bf16[256,128]{1,0:T(8,128)(2,1)} %param.3) | copy-start | bytes 196612
  10.0 712.8 %all-to-all-start = ((bf16[16,32,4096]{2,1,0:T(8,128)(2,1)}), bf16[16,32,4096]{2,1,0:T(8,128)(2,1)}, u32[]{:S(2)}, u32[]{:S(2)}) async-start(bf16[16,32,4096]{2,1,0:T(8,128)(2,1)} %stack.2), calls=%async_computation | async-start | bytes 8388608 | tf_op jit(solution)/shard_map/all_to_all | solution.py:29
  28.2 189.1 %all-gather.3.cloned.1.call-start = ((), (), s32[]{:S(2)}) async-start(), calls=%async_computation.1 | async-start | bytes 1114112 | tf_op jit(solution)/shard_map/all_gather | solution.py:20
  28.9 693.9 %all-gather.5.cloned.1.call-start = ((), (), s32[]{:S(2)}) async-start(), calls=%async_computation.2 | async-start | bytes 2162688 | tf_op jit(solution)/shard_map/all_gather | solution.py:25
  221.2 309.7 %copy-start = (bf16[4096,128]{1,0:T(8,128)(2,1)S(1)}, bf16[4096,128]{1,0:T(8,128)(2,1)}, u32[]{:S(2)}) copy-start(bf16[4096,128]{1,0:T(8,128)(2,1)} %all-gather.3.cloned.1.call-done) | copy-start | bytes 3145732
Sparse Core Ops, SparseCore 0:
  32.3 184.9 all-gather.2
  532.4 190.3 all-gather.4
